TPU v7x, 32 devices: a whole 2x2x4 slice. The times are simulated.
32 devices in a mesh: doc: 4 (over z), feat: 8 (over y, x, core).
Axes of the slice: x: 2, y: 2, z: 4, core: 2. Of those that a mesh axis runs over, the one named last changes fastest.
Arguments:
- documents: bfloat16 [512, 512], P('doc', 'feat'), may hold values from -6 to 6
- directions: bfloat16 [512, 32768], P('doc', 'feat'), may hold values from -0.5 to 0.5
- phase: float32 [32768], P('feat'), may hold values from -3.140625 to 3.140625
- amplitude: float32 [32768], P('feat'), may hold values from 0.4 to 2.3
- doc_weight: float32 [512], P('doc'), may hold values from 0.5 to 4.2
- labels: int32 [512], P('doc'), may hold values from 0 to 127
Outputs:
- margins: float32 [512, 128], P('doc')
- scaled_weights: float32 [32768, 128], P('feat')
All inputs are finite; a program needn't handle non-finite values.
Results may differ from a plain program's by a relative error of at most 0.0003.
Values may be sent and summed in bfloat16 or wider, within the bound.
A program may use at most 64 MiB of HBM per device.

v0:
```python
import jax
import jax.numpy as jnp
from jax import lax
from jax.sharding import PartitionSpec as P

C = 128
ITERS = 3
NEWTON = 3
HI = lax.Precision.HIGHEST
shrink_level = 0.1
ratio_floor = 1e-06


def logistic_prox(target, signs, weight_ratio):
    current = target
    for newton_step in range(NEWTON):
        chance = jax.nn.sigmoid(-signs * current)
        gradient = current - target - weight_ratio * signs * chance
        current = current - gradient / (1.0 + weight_ratio * chance * (1.0 - chance))
    return current


def shrink_values(target, limit):
    return target - jnp.clip(target, -limit, limit)


def per_device(documents, directions, phase, amplitude, doc_weight, labels):
    doc_count = documents.shape[0]
    width_tile = directions.shape[1]
    num_feat = lax.axis_size("feat")
    num_doc = lax.axis_size("doc")
    chunk = width_tile // num_doc
    row = lax.axis_index("doc")
    doc_rows = lax.all_gather(documents, "feat", axis=1, tiled=True)
    doc_full = lax.all_gather(doc_rows, "doc", axis=0, tiled=True)
    dir_chunk = lax.all_to_all(directions, "doc", split_axis=1, concat_axis=0, tiled=True)
    phase_c = lax.dynamic_slice_in_dim(phase, row * chunk, chunk, 0)
    amp_c = lax.dynamic_slice_in_dim(amplitude, row * chunk, chunk, 0)
    angles = jnp.dot(doc_full, dir_chunk, preferred_element_type=jnp.float32)
    features = jnp.sqrt(2.0 / width_tile) * amp_c * jnp.cos(angles + phase_c)
    blocks = features.reshape(num_doc, doc_count, chunk)
    gram = jnp.einsum("iac,ibc->iab", blocks, blocks, precision=HI)
    gram = lax.psum_scatter(gram, "doc", scatter_dimension=0, tiled=True)[0]
    eye = jnp.eye(doc_count, dtype=jnp.float32)
    factor = jnp.linalg.cholesky(eye + gram)
    lower_inv = lax.linalg.triangular_solve(factor, eye, left_side=True, lower=True)
    inverse = lax.dot_general(lower_inv, lower_inv, (((0,), (0,)), ((), ())), precision=HI)
    signs = jnp.where(labels[:, None] == jnp.arange(C, dtype=jnp.int32)[None, :], 1.0, -1.0).astype(
        jnp.float32
    )
    share_rows = doc_count // num_feat
    offset = lax.axis_index("feat") * share_rows
    signs = lax.dynamic_slice_in_dim(signs, offset, share_rows, 0)
    weight = lax.dynamic_slice_in_dim(doc_weight, offset, share_rows, 0)[:, None]
    rho = jnp.float32(1.0)
    margins = logistic_prox(jnp.zeros(signs.shape, jnp.float32), signs, weight / rho)
    sums = jnp.zeros(signs.shape, jnp.float32)
    duals_y = jnp.zeros(signs.shape, jnp.float32)
    part = jnp.zeros((doc_count, C), jnp.float32)
    image = jnp.zeros((doc_count, C), jnp.float32)
    weights = jnp.zeros((chunk, C), jnp.float32)
    product = jnp.zeros((doc_count, C), jnp.float32)
    for step in range(ITERS):
        correction = (margins - duals_y - sums) / num_feat
        correction = lax.all_gather(correction, "feat", axis=0, tiled=True)
        target = part + correction
        residue = target - image
        solved = jnp.dot(inverse, residue, precision=HI)
        applied = residue - solved
        part = target - solved
        sums = lax.psum_scatter(part, "feat", scatter_dimension=0, tiled=True)
        all_solved = lax.all_gather(solved, "doc", axis=0, tiled=True)
        lifted = lax.dot_general(features, all_solved, (((0,), (0,)), ((), ())), precision=HI)
        old_weights = weights
        old_margins = margins
        weights = shrink_values(weights + lifted / num_doc, shrink_level / (rho * num_doc))
        margins = logistic_prox(sums + duals_y, signs, weight / rho)
        duals_y = duals_y + sums - margins
        if step + 1 < ITERS:
            move = old_weights - weights
            if step == 0:
                d_move, d_solved, d_applied, d_lifted = (move, solved, applied, lifted)
            else:
                d_move = move - last_move / growth
                d_solved = solved - last_solved / growth
                d_applied = applied - last_applied / growth
                d_lifted = lifted - last_lifted / growth
            primal = (
                jnp.sum(num_doc * d_move * d_move + 2.0 * d_move * d_lifted)
                + jnp.sum(d_solved * d_applied)
                + jnp.sum((sums - margins) ** 2)
            )
            dual = num_doc * jnp.sum(move**2) + jnp.sum((margins - old_margins) ** 2)
            primal, dual = lax.psum((primal, dual), ("doc", "feat"))
            primal = jnp.maximum(primal, 0.0)
            new_product = jnp.dot(features, weights, precision=HI)
            new_product = lax.psum_scatter(new_product, "doc", scatter_dimension=0, tiled=True)
            growth = ((primal + ratio_floor) / (rho * rho * dual + ratio_floor)) ** 0.25
            rho = rho * growth
            duals_y = duals_y / growth
            image = new_product - (product - new_product + applied) / growth
            product = new_product
            last_move, last_solved, last_applied, last_lifted = (move, solved, applied, lifted)
    margins = lax.all_gather(margins, "feat", axis=0, tiled=True)
    weights = lax.all_gather(num_feat * weights, "doc", axis=0, tiled=True)
    return (margins, weights)


def solution(mesh):
    in_specs = (P("doc", "feat"), P("doc", "feat"), P("feat"), P("feat"), P("doc"), P("doc"))
    out_specs = (P("doc", None), P("feat", None))
    return jax.shard_map(
        per_device, mesh=mesh, in_specs=in_specs, out_specs=out_specs, check_vma=False
    )
```

profile of v0, /device:TPU:0, one launch (start us, length us, event | category | flops | bytes accessed | tf_op | source)
XLA Modules:
  0.0 383.9 jit_solution(2985545460666034803)
XLA Ops:
  9.4 6.3 %all-to-all-start = ((bf16[128,4,1024]{0,2,1:T(8,128)(2,1)}), bf16[128,4,1024]{0,2,1:T(8,128)(2,1)S(1)}, u32[]{:S(2)}, u32[]{:S(2)}) async-start(bf16[128,4,1024]{0,2,1:T(8,128)(2,1)} %bitcast), calls=%async_computation | async-start | bytes 2097152 | tf_op jit(solution)/shard_map/all_to_all | solution.py:36
  15.8 9.2 %all_gather.31 = bf16[128,512]{0,1:T(8,128)(2,1)S(1)} all-gather(bf16[128,64]{0,1:T(8,128)(2,1)S(1)} %copy-done.4), channel_id=1, replica_groups=mesh['doc'=4,'feat'=8] {'feat'}, dimensions={1}, use_global_device_ids=true | all-gather | bytes 147456 | tf_op jit(solution)/shard_map/all_gather | solution.py:34
  25.7 25.3 %all_gather.32 = bf16[512,512]{0,1:T(8,128)(2,1)} all-gather(bf16[128,512]{0,1:T(8,128)(2,1)S(1)} %all_gather.31), channel_id=1, replica_groups=mesh['doc'=4,'feat'=8] {'doc'}, dimensions={0}, use_global_device_ids=true | all-gather | bytes 655360 | tf_op jit(solution)/shard_map/all_gather | solution.py:35
  51.6 8.3 %cosine_multiply_fusion = f32[512,1024]{1,0:T(8,128)S(1)} fusion(bf16[512,512]{0,1:T(8,128)(2,1)} %all_gather.32, bf16[512,1024]{1,0:T(8,128)(2,1)S(1)} %bitcast.38, f32[1024]{0:T(1024)S(1)} %dynamic-slice-done, f32[1024]{0:T(1024)S(1)} %dynamic-slice_multiply_fusion), kind=kOutput, calls=%fused_computation | convolution fusion | flops 537919488 | bytes 3678208 | tf_op jit(solution)/shard_map/dot_general | solution.py:39
  63.1 9.4 %all_gather.30 = f32[128,128]{1,0:T(8,128)S(1)} all-gather(f32[16,128]{1,0:T(8,128)S(1)} %broadcast_multiply_fusion), channel_id=1, replica_groups=mesh['doc'=4,'feat'=8] {'feat'}, dimensions={0}, use_global_device_ids=true | all-gather | bytes 73728 | tf_op jit(solution)/shard_map/all_gather | solution.py:65
  72.5 14.2 %reduce-scatter.7.cloned.1.call-done = f32[1,128,128]{2,1,0:T(8,128)} async-done(((f32[4,128,128]{2,1,0:T(8,128)}), f32[1,128,128]{2,1,0:T(8,128)}) %reduce-scatter.7.cloned.1.call-update) | async-done | bytes 65552 | tf_op jit(solution)/shard_map/reduce_scatter | solution.py:43
  88.5 11.7 %cholesky.18 = f32[128,128]{1,0:T(8,128)S(1)} custom-call(f32[128,128]{1,0:T(8,128)S(1)} %fusion.13), custom_call_target="Cholesky" | custom-call | tf_op jit(solution)/shard_map/jit(cholesky)/cholesky | solution.py:45
  101.6 9.8 %custom-call.6 = f32[1,128,128]{1,2,0:T(8,128)S(1)} custom-call(f32[1,128,128]{2,1,0:T(8,128)S(1)} %fusion.10), custom_call_target="InvertDiagBlocksLowerTriangular" | custom-call | tf_op jit(solution)/shard_map/triangular_solve | solution.py:46
  113.5 14.1 %all_gather.33 = f32[512,128]{1,0:T(8,128)S(1)} all-gather(f32[128,128]{1,0:T(8,128)S(1)} %get-tuple-element.23), channel_id=1, replica_groups=mesh['doc'=4,'feat'=8] {'doc'}, dimensions={0}, use_global_device_ids=true | all-gather | bytes 327680 | tf_op jit(solution)/shard_map/all_gather | solution.py:72
  127.6 4.1 %multiply_reduce_fusion.1 = (f32[]{:T(128)}, f32[]{:T(128)}, f32[1024,128]{1,0:T(8,128)S(1)}) fusion(f32[512,1024]{1,0:T(8,128)S(1)} %cosine_multiply_fusion, f32[512,128]{1,0:T(8,128)S(1)} %all_gather.33), kind=kOutput, calls=%fused_computation.13 | convolution fusion | flops 806879232 | bytes 2883592 | tf_op jit(solution)/shard_map/dot_general | solution.py:73
  136.2 9.2 %reduce-scatter.9.cloned.1.call-done = f32[16,128]{1,0:T(8,128)} async-done(((f32[128,128]{1,0:T(8,128)}), f32[16,128]{1,0:T(8,128)}) %reduce-scatter.9.cloned.1.call-update) | async-done | bytes 8208 | tf_op jit(solution)/shard_map/reduce_scatter | solution.py:71
  149.3 39.3 %all-reduce.1 = (f32[]{:T(128)}, f32[]{:T(128)}) all-reduce(f32[]{:T(128)S(6)} %add.203, f32[]{:T(128)S(6)} %add.205), channel_id=1, replica_groups=mesh['doc'=4,'feat'=8] {'doc','feat'}, use_global_device_ids=true, to_apply=%region_7.8 | all-reduce | flops 2 | bytes 16 | tf_op jit(solution)/shard_map/psum | solution.py:94
  190.6 10.2 %all_gather.34 = f32[128,128]{1,0:T(8,128)S(1)} all-gather(f32[16,128]{1,0:T(8,128)S(1)} %subtract_multiply_fusion.2), channel_id=1, replica_groups=mesh['doc'=4,'feat'=8] {'feat'}, dimensions={0}, use_global_device_ids=true | all-gather | bytes 73728 | tf_op jit(solution)/shard_map/all_gather | solution.py:65
  203.2 14.2 %all_gather.35 = f32[512,128]{1,0:T(8,128)S(1)} all-gather(f32[128,128]{1,0:T(8,128)S(1)} %get-tuple-element.25), channel_id=1, replica_groups=mesh['doc'=4,'feat'=8] {'doc'}, dimensions={0}, use_global_device_ids=true | all-gather | bytes 327680 | tf_op jit(solution)/shard_map/all_gather | solution.py:72
  217.4 4.2 %multiply_reduce_fusion = (f32[]{:T(128)}, f32[]{:T(128)}, f32[1024,128]{1,0:T(8,128)S(1)}) fusion(f32[1024,128]{1,0:T(8,128)S(1)} %get-tuple-element.24, f32[]{:T(128)S(6)} %neg.66, f32[]{:T(128)S(6)} %div.199, f32[]{:T(128)S(6)} %pow.6, f32[512,1024]{1,0:T(8,128)S(1)} %cosine_multiply_fusion, f32[512,128]{1,0:T(8,128)S(1)} %all_gather.35), kind=kOutput, calls=%fused_computation.11 | convolution fusion | flops 808189952 | bytes 3407892 | tf_op jit(solution)/shard_map/dot_general | solution.py:73
  226.1 9.7 %reduce-scatter.13.cloned.1.call-done = f32[16,128]{1,0:T(8,128)} async-done(((f32[128,128]{1,0:T(8,128)}), f32[16,128]{1,0:T(8,128)}) %reduce-scatter.13.cloned.1.call-update) | async-done | bytes 8208 | tf_op jit(solution)/shard_map/reduce_scatter | solution.py:71
  238.5 39.4 %all-reduce = (f32[]{:T(128)}, f32[]{:T(128)}) all-reduce(f32[]{:T(128)S(6)} %add.219, f32[]{:T(128)S(6)} %add.221), channel_id=1, replica_groups=mesh['doc'=4,'feat'=8] {'doc','feat'}, use_global_device_ids=true, to_apply=%region_16.17 | all-reduce | flops 2 | bytes 16 | tf_op jit(solution)/shard_map/psum | solution.py:94
  279.9 11.2 %all_gather.36 = f32[128,128]{1,0:T(8,128)} all-gather(f32[16,128]{1,0:T(8,128)S(1)} %subtract_multiply_fusion.1), channel_id=1, replica_groups=mesh['doc'=4,'feat'=8] {'feat'}, dimensions={0}, use_global_device_ids=true | all-gather | bytes 73728 | tf_op jit(solution)/shard_map/all_gather | solution.py:65
  292.9 14.0 %all_gather.38 = f32[512,128]{1,0:T(8,128)S(1)} all-gather(f32[128,128]{1,0:T(8,128)S(1)} %get-tuple-element.28), channel_id=1, replica_groups=mesh['doc'=4,'feat'=8] {'doc'}, dimensions={0}, use_global_device_ids=true | all-gather | bytes 327680 | tf_op jit(solution)/shard_map/all_gather | solution.py:72
  306.9 4.2 %subtract_multiply_fusion = f32[1024,128]{1,0:T(8,128)} fusion(f32[512,1024]{1,0:T(8,128)S(1)} %cosine_multiply_fusion, f32[512,128]{1,0:T(8,128)S(1)} %all_gather.38, f32[]{:T(128)S(6)} %neg.70, f32[]{:T(128)S(6)} %div.220, f32[]{:T(128)S(6)} %neg.66, f32[]{:T(128)S(6)} %div.199, f32[1024,128]{1,0:T(8,128)S(1)} %get-tuple-element.26, ...), kind=kOutput, calls=%fused_computation.10 | convolution fusion | flops 807141376 | bytes 3932176 | tf_op jit(solution)/shard_map/dot_general | solution.py:73
  311.2 14.3 %reduce-scatter.17.cloned.1.call-done = f32[16,128]{1,0:T(8,128)} async-done(((f32[128,128]{1,0:T(8,128)}), f32[16,128]{1,0:T(8,128)}) %reduce-scatter.17.cloned.1.call-update) | async-done | bytes 8208 | tf_op jit(solution)/shard_map/reduce_scatter | solution.py:71
  326.4 9.2 %all_gather.37 = f32[128,128]{1,0:T(8,128)S(1)} all-gather(f32[16,128]{1,0:T(8,128)S(1)} %fusion.63), channel_id=1, replica_groups=mesh['doc'=4,'feat'=8] {'feat'}, dimensions={0}, use_global_device_ids=true | all-gather | bytes 73728 | tf_op jit(solution)/shard_map/all_gather | solution.py:104
  335.6 37.8 %all-gather.2.cloned.1.call-done = f32[4096,128]{1,0:T(8,128)} async-done(((f32[1024,128]{1,0:T(8,128)}), f32[4096,128]{1,0:T(8,128)}) %all-gather.2.cloned.1.call-update) | async-done | bytes 2097168 | tf_op jit(solution)/shard_map/all_gather | solution.py:105
  374.0 3.0 copy.16
  (69 shorter events, 28.5 us)
Async XLA Ops:
  7.2 8.6 %copy-start.4 = (bf16[128,64]{0,1:T(8,128)(2,1)S(1)}, bf16[128,64]{0,1:T(8,128)(2,1)}, u32[]{:S(2)}) copy-start(bf16[128,64]{0,1:T(8,128)(2,1)} %param.6) | copy-start | bytes 49156
  9.4 41.6 %all-to-all-start = ((bf16[128,4,1024]{0,2,1:T(8,128)(2,1)}), bf16[128,4,1024]{0,2,1:T(8,128)(2,1)S(1)}, u32[]{:S(2)}, u32[]{:S(2)}) async-start(bf16[128,4,1024]{0,2,1:T(8,128)(2,1)} %bitcast), calls=%async_computation | async-start | bytes 2097152 | tf_op jit(solution)/shard_map/all_to_all | solution.py:36
  15.8 70.9 %reduce-scatter.7.cloned.1.call-start = ((), (), s32[]{:S(2)}) async-start(), calls=%async_computation.7 | async-start | bytes 327680 | tf_op jit(solution)/shard_map/reduce_scatter | solution.py:43
  15.8 35.8 %dynamic-slice-start = ((f32[4096]{0:T(1024)}, s32[]{:T(128)}), f32[1024]{0:T(1024)S(1)}, s32[]{:S(2)}) async-start(f32[4096]{0:T(1024)} %param.8, s32[]{:T(128)} %select_n.18), calls=%async_computation.14 | async-start | bytes 8704 | tf_op jit(solution)/shard_map/dynamic_slice | solution.py:37
  59.9 2.9 copy-start.9
  59.9 2.9 copy-start.7
  62.7 82.6 %reduce-scatter.9.cloned.1.call-start = ((), (), s32[]{:S(2)}) async-start(), calls=%async_computation.8 | async-start | bytes 73728 | tf_op jit(solution)/shard_map/reduce_scatter | solution.py:71
  62.9 173.0 %copy-start.5 = (s32[16]{0:T(128)}, s32[16]{0:T(128)S(1)}, u32[]{:S(2)}) copy-start(s32[16]{0:T(128)S(1)} %dynamic-slice) | copy-start | bytes 196
  113.5 87.4 %reduce-scatter.11.cloned.1.call-start = ((), (), s32[]{:S(2)}) async-start(), calls=%async_computation.9 | async-start | bytes 327680 | tf_op jit(solution)/shard_map/reduce_scatter | solution.py:97
  131.7 69.2 %copy-start = (f32[128,128]{1,0:T(8,128)S(1)}, f32[128,128]{1,0:T(8,128)}, u32[]{:S(2)}) copy-start(f32[128,128]{1,0:T(8,128)} %get-tuple-element.20) | copy-start | bytes 196612
  136.1 99.8 %reduce-scatter.13.cloned.1.call-start = ((), (), s32[]{:S(2)}) async-start(), calls=%async_computation.10 | async-start | bytes 73728 | tf_op jit(solution)/shard_map/reduce_scatter | solution.py:71
  203.2 87.9 %reduce-scatter.15.cloned.1.call-start = ((), (), s32[]{:S(2)}) async-start(), calls=%async_computation.11 | async-start | bytes 327680 | tf_op jit(solution)/shard_map/reduce_scatter | solution.py:97
  221.6 69.5 %copy-start.1 = (f32[128,128]{1,0:T(8,128)S(1)}, f32[128,128]{1,0:T(8,128)}, u32[]{:S(2)}) copy-start(f32[128,128]{1,0:T(8,128)} %reduce-scatter.11.cloned.1.call-done) | copy-start | bytes 196612
  221.6 69.5 %copy-start.2 = (f32[128,128]{1,0:T(8,128)S(1)}, f32[128,128]{1,0:T(8,128)}, u32[]{:S(2)}) copy-start(f32[128,128]{1,0:T(8,128)} %get-tuple-element.22) | copy-start | bytes 196612
  224.2 101.4 %reduce-scatter.17.cloned.1.call-start = ((), (), s32[]{:S(2)}) async-start(), calls=%async_computation.12 | async-start | bytes 73728 | tf_op jit(solution)/shard_map/reduce_scatter | solution.py:71
  292.9 80.5 %all-gather.2.cloned.1.call-start = ((), (), s32[]{:S(2)}) async-start(), calls=%async_computation.13 | async-start | bytes 2621440 | tf_op jit(solution)/shard_map/all_gather | solution.py:105
  306.9 4.3 %copy-start.8 = (f32[128]{0:T(128)S(1)}, f32[128]{0:T(128)}, u32[]{:S(2)}) copy-start(f32[128]{0:T(128)} %param.10) | copy-start | bytes 1540
  306.9 18.7 %copy-start.3 = (f32[16,128]{1,0:T(8,128)S(1)}, f32[16,128]{1,0:T(8,128)}, u32[]{:S(2)}) copy-start(f32[16,128]{1,0:T(8,128)} %reduce-scatter.13.cloned.1.call-done) | copy-start | bytes 24580
  306.9 18.7 %copy-start.6 = (s32[16]{0:T(128)S(1)}, s32[16]{0:T(128)}, u32[]{:S(2)}) copy-start(s32[16]{0:T(128)} %copy-done.5) | copy-start | bytes 196
Sparse Core Ops, SparseCore 0:
  62.8 23.8 reduce-scatter.6
  113.6 31.7 reduce-scatter.8
  148.2 19.9 reduce-scatter.10
  203.3 32.4 reduce-scatter.12
  238.5 19.9 reduce-scatter.14
  293.0 32.5 reduce-scatter.16
  327.7 45.6 all-gather.1
where the time goes:
time: 385 us; the launch traced here: 384 us
  blocking collectives  195 us (51%)
  waiting for transfers between devices  85.3 us (22%)
  matrix products  33.9 us (9%)
  other arithmetic  32.9 us (9%)
  between operations  23 us (6%)
  local copies, waits for them, and re-layouts  6.75 us (2%)
  starting transfers between devices  6.6 us (2%)
    psum x2, blocking collectives, per_device(): primal, dual = lax.psum((primal, dual), ('doc', 'feat'))  78.7 us
    all_gather x3, blocking collectives, per_device(): all_solved = lax.all_gather(solved, 'doc', axis=0, tiled=True)  42.2 us
    all_gather x1, waiting for transfers between devices, per_device(): weights = lax.all_gather(num_feat * weights, 'doc', axis=0, tiled=True)  37.8 us
    reduce_scatter x3, waiting for transfers between devices, per_device(): sums = lax.psum_scatter(part, 'feat', scatter_dimension=0, tiled=True)  33.2 us
    all_gather x3, blocking collectives, per_device(): correction = lax.all_gather(correction, 'feat', axis=0, tiled=True)  30.8 us
    all_gather x1, blocking collectives, per_device(): doc_full = lax.all_gather(doc_rows, 'doc', axis=0, tiled=True)  25.3 us
    reduce_scatter x1, waiting for transfers between devices, per_device(): gram = lax.psum_scatter(gram, 'doc', scatter_dimension=0, tiled=True)[0]  14.2 us
    dot_general x3, matrix products, per_device(): lax.dot_general(features, all_solved, (((0,), (0,)), ((), ())), precision...  12.5 us
  transfers between devices with their start and end apart: 8, of which 5 were waited for; matrix products, arithmetic and copies ran while one was open for 7% of the time, Pallas kernels for 0%

commit v1 on v0

--- a/solution.py
+++ b/solution.py
@@ -9,6 +9,11 @@
 HI = lax.Precision.HIGHEST
 shrink_level = 0.1
 ratio_floor = 1e-06
+
+
+def by_each_axis(value, inner_axis, outer_axis):
+    partial = lax.psum(value, inner_axis)
+    return lax.psum(partial, outer_axis)
 
 
 def logistic_prox(target, signs, weight_ratio):
@@ -91,7 +96,7 @@
                 + jnp.sum((sums - margins) ** 2)
             )
             dual = num_doc * jnp.sum(move**2) + jnp.sum((margins - old_margins) ** 2)
-            primal, dual = lax.psum((primal, dual), ("doc", "feat"))
+            primal, dual = by_each_axis((primal, dual), "feat", "doc")
             primal = jnp.maximum(primal, 0.0)
             new_product = jnp.dot(features, weights, precision=HI)
             new_product = lax.psum_scatter(new_product, "doc", scatter_dimension=0, tiled=True)

time: 385 us -> 351 us (0.912)
  blocking collectives: 195 us -> 166 us
  waiting for transfers between devices: 85.3 us -> 80.9 us
    psum x2 -> x4, blocking collectives: 78.7 us -> 50.1 us  [the longest x2 25.8 us: by_each_axis(): partial = lax.psum(value, inner_axis)]
    reduce_scatter x3, waiting for transfers between devices: 33.2 us -> 28.8 us  [per_device(): sums = lax.psum_scatter(part, 'feat', scatter_dimension=0, tiled=True)]
where the time goes in v1:
time: 351 us; the launch traced here: 350 us
  blocking collectives  166 us (47%)
  waiting for transfers between devices  80.9 us (23%)
  matrix products  33.9 us (10%)
  other arithmetic  32.9 us (9%)
  between operations  23.2 us (7%)
  starting transfers between devices  6.86 us (2%)
  local copies, waits for them, and re-layouts  6.75 us (2%)
    all_gather x3, blocking collectives, per_device(): all_solved = lax.all_gather(solved, 'doc', axis=0, tiled=True)  42.9 us
    all_gather x1, waiting for transfers between devices, per_device(): weights = lax.all_gather(num_feat * weights, 'doc', axis=0, tiled=True)  37.8 us
    all_gather x3, blocking collectives, per_device(): correction = lax.all_gather(correction, 'feat', axis=0, tiled=True)  28.8 us
    reduce_scatter x3, waiting for transfers between devices, per_device(): sums = lax.psum_scatter(part, 'feat', scatter_dimension=0, tiled=True)  28.8 us
    psum x2, blocking collectives, by_each_axis(): partial = lax.psum(value, inner_axis)  25.8 us
    all_gather x1, blocking collectives, per_device(): doc_full = lax.all_gather(doc_rows, 'doc', axis=0, tiled=True)  25.3 us
    psum x2, blocking collectives, by_each_axis(): return lax.psum(partial, outer_axis)  24.3 us
    reduce_scatter x1, waiting for transfers between devices, per_device(): gram = lax.psum_scatter(gram, 'doc', scatter_dimension=0, tiled=True)[0]  14.2 us
  transfers between devices with their start and end apart: 8, of which 5 were waited for; matrix products, arithmetic and copies ran while one was open for 7% of the time, Pallas kernels for 0%

profile of v1, /device:TPU:0, one launch (start us, length us, event | category | flops | bytes accessed | tf_op | source)
XLA Modules:
  0.0 350.1 jit_solution(849150581545633026)
XLA Ops:
  9.4 6.3 %all-to-all-start = ((bf16[128,4,1024]{0,2,1:T(8,128)(2,1)}), bf16[128,4,1024]{0,2,1:T(8,128)(2,1)S(1)}, u32[]{:S(2)}, u32[]{:S(2)}) async-start(bf16[128,4,1024]{0,2,1:T(8,128)(2,1)} %bitcast), calls=%async_computation | async-start | bytes 2097152 | tf_op jit(solution)/shard_map/all_to_all | solution.py:41
  15.8 9.2 %all_gather.31 = bf16[128,512]{0,1:T(8,128)(2,1)S(1)} all-gather(bf16[128,64]{0,1:T(8,128)(2,1)S(1)} %copy-done.4), channel_id=1, replica_groups=mesh['doc'=4,'feat'=8] {'feat'}, dimensions={1}, use_global_device_ids=true | all-gather | bytes 147456 | tf_op jit(solution)/shard_map/all_gather | solution.py:39
  25.7 25.3 %all_gather.32 = bf16[512,512]{0,1:T(8,128)(2,1)} all-gather(bf16[128,512]{0,1:T(8,128)(2,1)S(1)} %all_gather.31), channel_id=1, replica_groups=mesh['doc'=4,'feat'=8] {'doc'}, dimensions={0}, use_global_device_ids=true | all-gather | bytes 655360 | tf_op jit(solution)/shard_map/all_gather | solution.py:40
  51.6 8.3 %cosine_multiply_fusion = f32[512,1024]{1,0:T(8,128)S(1)} fusion(bf16[512,512]{0,1:T(8,128)(2,1)} %all_gather.32, bf16[512,1024]{1,0:T(8,128)(2,1)S(1)} %bitcast.38, f32[1024]{0:T(1024)S(1)} %dynamic-slice-done, f32[1024]{0:T(1024)S(1)} %dynamic-slice_multiply_fusion), kind=kOutput, calls=%fused_computation | convolution fusion | flops 537919488 | bytes 3678208 | tf_op jit(solution)/shard_map/dot_general | solution.py:44
  63.1 9.4 %all_gather.30 = f32[128,128]{1,0:T(8,128)S(1)} all-gather(f32[16,128]{1,0:T(8,128)S(1)} %broadcast_multiply_fusion), channel_id=1, replica_groups=mesh['doc'=4,'feat'=8] {'feat'}, dimensions={0}, use_global_device_ids=true | all-gather | bytes 73728 | tf_op jit(solution)/shard_map/all_gather | solution.py:70
  72.5 14.2 %reduce-scatter.7.cloned.1.call-done = f32[1,128,128]{2,1,0:T(8,128)} async-done(((f32[4,128,128]{2,1,0:T(8,128)}), f32[1,128,128]{2,1,0:T(8,128)}) %reduce-scatter.7.cloned.1.call-update) | async-done | bytes 65552 | tf_op jit(solution)/shard_map/reduce_scatter | solution.py:48
  88.5 11.7 %cholesky.18 = f32[128,128]{1,0:T(8,128)S(1)} custom-call(f32[128,128]{1,0:T(8,128)S(1)} %fusion.13), custom_call_target="Cholesky" | custom-call | tf_op jit(solution)/shard_map/jit(cholesky)/cholesky | solution.py:50
  101.6 9.8 %custom-call.6 = f32[1,128,128]{1,2,0:T(8,128)S(1)} custom-call(f32[1,128,128]{2,1,0:T(8,128)S(1)} %fusion.10), custom_call_target="InvertDiagBlocksLowerTriangular" | custom-call | tf_op jit(solution)/shard_map/triangular_solve | solution.py:51
  113.5 14.1 %all_gather.33 = f32[512,128]{1,0:T(8,128)S(1)} all-gather(f32[128,128]{1,0:T(8,128)S(1)} %get-tuple-element.27), channel_id=1, replica_groups=mesh['doc'=4,'feat'=8] {'doc'}, dimensions={0}, use_global_device_ids=true | all-gather | bytes 327680 | tf_op jit(solution)/shard_map/all_gather | solution.py:77
  136.2 9.2 %reduce-scatter.9.cloned.1.call-done = f32[16,128]{1,0:T(8,128)} async-done(((f32[128,128]{1,0:T(8,128)}), f32[16,128]{1,0:T(8,128)}) %reduce-scatter.9.cloned.1.call-update) | async-done | bytes 8208 | tf_op jit(solution)/shard_map/reduce_scatter | solution.py:76
  149.3 13.1 %all-reduce.1 = (f32[]{:T(128)}, f32[]{:T(128)}) all-reduce(f32[]{:T(128)S(6)} %add.211, f32[]{:T(128)S(6)} %add.213), channel_id=1, replica_groups=mesh['doc'=4,'feat'=8] {'feat'}, use_global_device_ids=true, to_apply=%region_7.8 | all-reduce | flops 2 | bytes 16 | tf_op jit(solution)/shard_map/psum | solution.py:15
  162.4 12.0 %all-reduce.3 = (f32[]{:T(128)}, f32[]{:T(128)}) all-reduce(f32[]{:T(128)} %get-tuple-element.10, f32[]{:T(128)} %get-tuple-element.11), channel_id=1, replica_groups=mesh['doc'=4,'feat'=8] {'doc'}, use_global_device_ids=true, to_apply=%region_8.9 | all-reduce | flops 2 | bytes 16 | tf_op jit(solution)/shard_map/psum | solution.py:16
  176.4 9.2 %all_gather.34 = f32[128,128]{1,0:T(8,128)S(1)} all-gather(f32[16,128]{1,0:T(8,128)S(1)} %subtract_multiply_fusion.2), channel_id=1, replica_groups=mesh['doc'=4,'feat'=8] {'feat'}, dimensions={0}, use_global_device_ids=true | all-gather | bytes 73728 | tf_op jit(solution)/shard_map/all_gather | solution.py:70
  188.0 14.4 %all_gather.35 = f32[512,128]{1,0:T(8,128)S(1)} all-gather(f32[128,128]{1,0:T(8,128)S(1)} %get-tuple-element.29), channel_id=1, replica_groups=mesh['doc'=4,'feat'=8] {'doc'}, dimensions={0}, use_global_device_ids=true | all-gather | bytes 327680 | tf_op jit(solution)/shard_map/all_gather | solution.py:77
  202.4 4.2 %multiply_reduce_fusion = (f32[]{:T(128)}, f32[]{:T(128)}, f32[1024,128]{1,0:T(8,128)S(1)}) fusion(f32[1024,128]{1,0:T(8,128)S(1)} %get-tuple-element.28, f32[]{:T(128)S(6)} %neg.66, f32[]{:T(128)S(6)} %div.199, f32[]{:T(128)S(6)} %pow.6, f32[512,1024]{1,0:T(8,128)S(1)} %cosine_multiply_fusion, f32[512,128]{1,0:T(8,128)S(1)} %all_gather.35), kind=kOutput, calls=%fused_computation.11 | convolution fusion | flops 808189952 | bytes 3407892 | tf_op jit(solution)/shard_map/dot_general | solution.py:78
  211.4 7.5 %reduce-scatter.13.cloned.1.call-done = f32[16,128]{1,0:T(8,128)} async-done(((f32[128,128]{1,0:T(8,128)}), f32[16,128]{1,0:T(8,128)}) %reduce-scatter.13.cloned.1.call-update) | async-done | bytes 8208 | tf_op jit(solution)/shard_map/reduce_scatter | solution.py:76
  221.6 12.7 %all-reduce = (f32[]{:T(128)}, f32[]{:T(128)}) all-reduce(f32[]{:T(128)S(6)} %add.227, f32[]{:T(128)S(6)} %add.229), channel_id=1, replica_groups=mesh['doc'=4,'feat'=8] {'feat'}, use_global_device_ids=true, to_apply=%region_18.19 | all-reduce | flops 2 | bytes 16 | tf_op jit(solution)/shard_map/psum | solution.py:15
  234.3 12.4 %all-reduce.2 = (f32[]{:T(128)}, f32[]{:T(128)}) all-reduce(f32[]{:T(128)} %get-tuple-element.8, f32[]{:T(128)} %get-tuple-element.9), channel_id=1, replica_groups=mesh['doc'=4,'feat'=8] {'doc'}, use_global_device_ids=true, to_apply=%region_19.20 | all-reduce | flops 2 | bytes 16 | tf_op jit(solution)/shard_map/psum | solution.py:16
  248.8 10.2 %all_gather.36 = f32[128,128]{1,0:T(8,128)} all-gather(f32[16,128]{1,0:T(8,128)S(1)} %subtract_multiply_fusion.1), channel_id=1, replica_groups=mesh['doc'=4,'feat'=8] {'feat'}, dimensions={0}, use_global_device_ids=true | all-gather | bytes 73728 | tf_op jit(solution)/shard_map/all_gather | solution.py:70
  260.8 14.4 %all_gather.38 = f32[512,128]{1,0:T(8,128)S(1)} all-gather(f32[128,128]{1,0:T(8,128)S(1)} %get-tuple-element.32), channel_id=1, replica_groups=mesh['doc'=4,'feat'=8] {'doc'}, dimensions={0}, use_global_device_ids=true | all-gather | bytes 327680 | tf_op jit(solution)/shard_map/all_gather | solution.py:77
  275.2 4.2 %subtract_multiply_fusion = f32[1024,128]{1,0:T(8,128)} fusion(f32[512,1024]{1,0:T(8,128)S(1)} %cosine_multiply_fusion, f32[512,128]{1,0:T(8,128)S(1)} %all_gather.38, f32[]{:T(128)S(6)} %neg.70, f32[]{:T(128)S(6)} %div.220, f32[]{:T(128)S(6)} %neg.66, f32[]{:T(128)S(6)} %div.199, f32[1024,128]{1,0:T(8,128)S(1)} %get-tuple-element.30, ...), kind=kOutput, calls=%fused_computation.10 | convolution fusion | flops 807141376 | bytes 3932176 | tf_op jit(solution)/shard_map/dot_general | solution.py:78
  279.6 12.1 %reduce-scatter.17.cloned.1.call-done = f32[16,128]{1,0:T(8,128)} async-done(((f32[128,128]{1,0:T(8,128)}), f32[16,128]{1,0:T(8,128)}) %reduce-scatter.17.cloned.1.call-update) | async-done | bytes 8208 | tf_op jit(solution)/shard_map/reduce_scatter | solution.py:76
  292.6 9.2 %all_gather.37 = f32[128,128]{1,0:T(8,128)S(1)} all-gather(f32[16,128]{1,0:T(8,128)S(1)} %fusion.63), channel_id=1, replica_groups=mesh['doc'=4,'feat'=8] {'feat'}, dimensions={0}, use_global_device_ids=true | all-gather | bytes 73728 | tf_op jit(solution)/shard_map/all_gather | solution.py:109
  301.8 37.8 %all-gather.2.cloned.1.call-done = f32[4096,128]{1,0:T(8,128)} async-done(((f32[1024,128]{1,0:T(8,128)}), f32[4096,128]{1,0:T(8,128)}) %all-gather.2.cloned.1.call-update) | async-done | bytes 2097168 | tf_op jit(solution)/shard_map/all_gather | solution.py:110
  (71 shorter events, 35.9 us)
Async XLA Ops:
  7.2 8.6 %copy-start.4 = (bf16[128,64]{0,1:T(8,128)(2,1)S(1)}, bf16[128,64]{0,1:T(8,128)(2,1)}, u32[]{:S(2)}) copy-start(bf16[128,64]{0,1:T(8,128)(2,1)} %param.6) | copy-start | bytes 49156
  9.4 41.6 %all-to-all-start = ((bf16[128,4,1024]{0,2,1:T(8,128)(2,1)}), bf16[128,4,1024]{0,2,1:T(8,128)(2,1)S(1)}, u32[]{:S(2)}, u32[]{:S(2)}) async-start(bf16[128,4,1024]{0,2,1:T(8,128)(2,1)} %bitcast), calls=%async_computation | async-start | bytes 2097152 | tf_op jit(solution)/shard_map/all_to_all | solution.py:41
  15.8 70.9 %reduce-scatter.7.cloned.1.call-start = ((), (), s32[]{:S(2)}) async-start(), calls=%async_computation.7 | async-start | bytes 327680 | tf_op jit(solution)/shard_map/reduce_scatter | solution.py:48
  15.8 35.8 %dynamic-slice-start = ((f32[4096]{0:T(1024)}, s32[]{:T(128)}), f32[1024]{0:T(1024)S(1)}, s32[]{:S(2)}) async-start(f32[4096]{0:T(1024)} %param.8, s32[]{:T(128)} %select_n.18), calls=%async_computation.14 | async-start | bytes 8704 | tf_op jit(solution)/shard_map/dynamic_slice | solution.py:42
  59.9 2.9 copy-start.9
  59.9 2.9 copy-start.7
  62.7 82.6 %reduce-scatter.9.cloned.1.call-start = ((), (), s32[]{:S(2)}) async-start(), calls=%async_computation.8 | async-start | bytes 73728 | tf_op jit(solution)/shard_map/reduce_scatter | solution.py:76
  62.9 156.1 %copy-start.5 = (s32[16]{0:T(128)}, s32[16]{0:T(128)S(1)}, u32[]{:S(2)}) copy-start(s32[16]{0:T(128)S(1)} %dynamic-slice) | copy-start | bytes 196
  113.5 72.2 %reduce-scatter.11.cloned.1.call-start = ((), (), s32[]{:S(2)}) async-start(), calls=%async_computation.9 | async-start | bytes 327680 | tf_op jit(solution)/shard_map/reduce_scatter | solution.py:102
  131.7 54.0 %copy-start = (f32[128,128]{1,0:T(8,128)S(1)}, f32[128,128]{1,0:T(8,128)}, u32[]{:S(2)}) copy-start(f32[128,128]{1,0:T(8,128)} %get-tuple-element.24) | copy-start | bytes 196612
  136.1 82.8 %reduce-scatter.13.cloned.1.call-start = ((), (), s32[]{:S(2)}) async-start(), calls=%async_computation.10 | async-start | bytes 73728 | tf_op jit(solution)/shard_map/reduce_scatter | solution.py:76
  188.0 71.0 %reduce-scatter.15.cloned.1.call-start = ((), (), s32[]{:S(2)}) async-start(), calls=%async_computation.11 | async-start | bytes 327680 | tf_op jit(solution)/shard_map/reduce_scatter | solution.py:102
  206.6 52.4 %copy-start.1 = (f32[128,128]{1,0:T(8,128)S(1)}, f32[128,128]{1,0:T(8,128)}, u32[]{:S(2)}) copy-start(f32[128,128]{1,0:T(8,128)} %reduce-scatter.11.cloned.1.call-done) | copy-start | bytes 196612
  206.6 52.4 %copy-start.2 = (f32[128,128]{1,0:T(8,128)S(1)}, f32[128,128]{1,0:T(8,128)}, u32[]{:S(2)}) copy-start(f32[128,128]{1,0:T(8,128)} %get-tuple-element.26) | copy-start | bytes 196612
  209.2 82.5 %reduce-scatter.17.cloned.1.call-start = ((), (), s32[]{:S(2)}) async-start(), calls=%async_computation.12 | async-start | bytes 73728 | tf_op jit(solution)/shard_map/reduce_scatter | solution.py:76
  260.8 78.8 %all-gather.2.cloned.1.call-start = ((), (), s32[]{:S(2)}) async-start(), calls=%async_computation.13 | async-start | bytes 2621440 | tf_op jit(solution)/shard_map/all_gather | solution.py:110
  275.2 4.3 %copy-start.8 = (f32[128]{0:T(128)S(1)}, f32[128]{0:T(128)}, u32[]{:S(2)}) copy-start(f32[128]{0:T(128)} %param.10) | copy-start | bytes 1540
  275.2 16.5 %copy-start.3 = (f32[16,128]{1,0:T(8,128)S(1)}, f32[16,128]{1,0:T(8,128)}, u32[]{:S(2)}) copy-start(f32[16,128]{1,0:T(8,128)} %reduce-scatter.13.cloned.1.call-done) | copy-start | bytes 24580
  275.2 16.5 %copy-start.6 = (s32[16]{0:T(128)S(1)}, s32[16]{0:T(128)}, u32[]{:S(2)}) copy-start(s32[16]{0:T(128)} %copy-done.5) | copy-start | bytes 196
Sparse Core Ops, SparseCore 0:
  62.8 23.8 reduce-scatter.6
  113.6 31.7 reduce-scatter.8
  148.2 19.9 reduce-scatter.10
  188.1 30.7 reduce-scatter.12
  221.6 19.9 reduce-scatter.14
  260.9 30.7 reduce-scatter.16
  293.9 45.6 all-gather.1
